TPU v7x, 32 devices: a whole 2x2x4 slice. The times are simulated.
32 devices in a mesh: region: 2 (over y), tile: 4 (over z), member: 2 (over x), date: 2 (over core).
Axes of the slice: x: 2, y: 2, z: 4, core: 2. Of those that a mesh axis runs over, the one named last changes fastest.
Arguments:
- sim_lai: bfloat16 [2, 32, 4, 32, 512], P('date', ('region', 'tile'), 'member'), parts along dimension 1, may hold values from 0 to 6
- owner_ids: int32 [2, 32], P('date', ('region', 'tile')), parts along dimension 1, may hold values from 0 to 3, as said below
- cloud_words: int32 [2, 32, 32], P('date', ('region', 'tile')), parts along dimension 1, may hold values from -2147483648 to 2147483646
- scene_lai: bfloat16 [2, 8, 8, 16, 256], P('date', ('region', 'tile'), 'member'), parts along dimension 1, may hold values from 0 to 6
- scene_sigma: bfloat16 [2, 8, 8, 16, 256], P('date', ('region', 'tile'), 'member'), parts along dimension 1, may hold values from 1 to 4
- mtf_taps: float32 [2, 7], replicated, may hold values from 0.1 to 1
Outputs:
- lai_update: bfloat16 [2, 32, 4, 32, 512], P('date', ('region', 'tile'), 'member'), parts along dimension 1
There are 2 independent parts, one for each index of `region`. A program takes and returns all parts, laid end to end along the dimension named above; an argument that names none is the same for every part. Nothing has to cross between parts.
Inputs may be any that keep to these rules, and one draw needn't show every extreme that they name: `owner_ids`: on each date each device along tile, holding 4 consecutive tiles, sends either none or exactly 2 of them to each owner; some owner receives 2 tiles from every device.
All inputs are finite; a program needn't handle non-finite values.
Results may differ from a plain program's by a relative error of at most 0.013.
The roundings to bfloat16 on the way count: a program that leaves them out, or rounds other values in their place, can miss the bound.
Values may be sent and summed in bfloat16 or wider, within the bound.
No kernel may reach another device: no remote copies, remote signals or barrier semaphores. Data moves between devices by JAX's collectives and lax.ppermute only.
A program may use at most 64 MiB of HBM per device.

v0:
```python
import jax
import jax.numpy as jnp
from jax import lax
from jax.sharding import PartitionSpec as P

CAP = 2


def band_tables(mtf_taps, tile_rows, tile_cols):
    kernel = mtf_taps / jnp.sum(mtf_taps, axis=1, keepdims=True)
    half_rows = tile_rows // 2
    half_cols = tile_cols // 2
    tap_reach = mtf_taps.shape[1] // 2
    out_rows = lax.broadcasted_iota(jnp.int32, (half_rows, tile_rows), 0)
    in_rows = lax.broadcasted_iota(jnp.int32, (half_rows, tile_rows), 1)
    in_cols = lax.broadcasted_iota(jnp.int32, (tile_cols, half_cols), 0)
    out_cols = lax.broadcasted_iota(jnp.int32, (tile_cols, half_cols), 1)
    row_table = jnp.zeros((half_rows, tile_rows), jnp.float32)
    col_table = jnp.zeros((tile_cols, half_cols), jnp.float32)
    for offset in range(mtf_taps.shape[1]):
        row_table = row_table + jnp.where(
            in_rows == 2 * out_rows + offset - tap_reach, kernel[0, offset], 0.0
        )
        col_table = col_table + jnp.where(
            in_cols == 2 * out_cols + offset - tap_reach, kernel[1, offset], 0.0
        )
    return (row_table.astype(jnp.bfloat16), col_table.astype(jnp.bfloat16))


def cloud_weights(words, half_rows, half_cols):
    shifts = jnp.arange(32)
    bit_values = jnp.bitwise_and(jnp.right_shift(words[..., None], shifts), 1)
    cells = bit_values.reshape(words.shape[:-1] + (half_rows // 2, half_cols // 2)).astype(
        jnp.float32
    )
    return jnp.repeat(jnp.repeat(cells, 2, axis=-2), 2, axis=-1)


def weighted_misfit(valid, observed, sigma_obs, predicted):
    sigma_wide = sigma_obs.astype(jnp.float32)
    gap = observed.astype(jnp.float32) - predicted.astype(jnp.float32)
    return (valid * gap / (sigma_wide * sigma_wide)).astype(jnp.bfloat16)


def degrade(fields, row_table, col_table):
    blurred = jnp.einsum(
        "ir,...rc->...ic", row_table, fields, preferred_element_type=jnp.float32
    ).astype(jnp.bfloat16)
    return jnp.einsum(
        "...ic,cj->...ij", blurred, col_table, preferred_element_type=jnp.float32
    ).astype(jnp.bfloat16)


def adjoint_map(misfit, row_table, col_table):
    spread = jnp.einsum(
        "...ij,cj->...ic", misfit, col_table, preferred_element_type=jnp.float32
    ).astype(jnp.bfloat16)
    return jnp.einsum(
        "ir,...ic->...rc", row_table, spread, preferred_element_type=jnp.float32
    ).astype(jnp.bfloat16)


def per_device(sim_lai, owner_ids, cloud_words, scene_lai, scene_sigma, mtf_taps):
    tile_count = lax.axis_size("tile")
    tiles_here = sim_lai.shape[1]
    members_here = sim_lai.shape[2]
    tile_rows = sim_lai.shape[3]
    tile_cols = sim_lai.shape[4]
    half_rows = tile_rows // 2
    half_cols = tile_cols // 2
    slot_count = tile_count * CAP
    row_table, col_table = band_tables(mtf_taps, tile_rows, tile_cols)
    owners = owner_ids[0]
    same_owner = owners[:, None] == owners[None, :]
    earlier = lax.broadcasted_iota(jnp.int32, (tiles_here, tiles_here), 0) < lax.broadcasted_iota(
        jnp.int32, (tiles_here, tiles_here), 1
    )
    rank = jnp.sum(jnp.logical_and(same_owner, earlier).astype(jnp.int32), axis=0)
    target = owners * CAP + rank
    slot_onehot = lax.broadcasted_iota(jnp.int32, (slot_count, tiles_here), 0) == target[None, :]
    onehot_bf = slot_onehot.astype(jnp.bfloat16)
    scenes, sigmas = (
        lax.all_gather(scene_lai, "member", axis=2, tiled=True),
        lax.all_gather(scene_sigma, "member", axis=2, tiled=True),
    )
    local_tiles = sim_lai[0]
    words_out = jnp.sum(jnp.where(slot_onehot[:, :, None], cloud_words[0][None, :, :], 0), axis=1)
    words_out = words_out.reshape(tile_count, CAP, -1)
    scenes = scenes.reshape(slot_count, 1, half_rows, half_cols)
    sigmas = sigmas.reshape(slot_count, 1, half_rows, half_cols)
    flat = local_tiles.reshape(tiles_here, -1)
    outgoing = (
        jnp.dot(onehot_bf, flat, preferred_element_type=jnp.float32)
        .astype(jnp.bfloat16)
        .reshape(tile_count, CAP, members_here, tile_rows, tile_cols)
    )
    arrived, arrived_words = (
        lax.all_to_all(outgoing, "tile", split_axis=0, concat_axis=0, tiled=True),
        lax.all_to_all(words_out, "tile", split_axis=0, concat_axis=0, tiled=True),
    )
    arrived = arrived.reshape(slot_count, members_here, tile_rows, tile_cols)
    valid = cloud_weights(arrived_words.reshape(slot_count, -1), half_rows, half_cols)[:, None]
    misfit = weighted_misfit(valid, scenes, sigmas, degrade(arrived, row_table, col_table))
    answered = adjoint_map(misfit, row_table, col_table).reshape(
        tile_count, CAP, members_here, tile_rows, tile_cols
    )
    returned = lax.all_to_all(answered, "tile", split_axis=0, concat_axis=0, tiled=True)
    flat = returned.reshape(slot_count, -1)
    lai_update = (
        jnp.dot(onehot_bf.T, flat, preferred_element_type=jnp.float32)
        .astype(jnp.bfloat16)
        .reshape(tiles_here, members_here, tile_rows, tile_cols)
    )
    return lai_update[None]


def solution(mesh):
    placed = (
        P("date", ("region", "tile"), "member", None, None),
        P("date", ("region", "tile")),
        P("date", ("region", "tile"), None),
        P("date", ("region", "tile"), "member", None, None),
        P("date", ("region", "tile"), "member", None, None),
        P(),
    )
    return jax.shard_map(
        per_device,
        mesh=mesh,
        in_specs=placed,
        out_specs=P("date", ("region", "tile"), "member", None, None),
        check_vma=False,
    )
```

profile of v0, /device:TPU:0, one launch (start us, length us, event | category | flops | bytes accessed | tf_op | source)
XLA Modules:
  0.0 74.5 jit_solution(14291288457161708068)
XLA Ops:
  0.0 0.0 copy-start.4
  0.0 0.7 copy-done.4
  0.7 0.1 convert_reduce_fusion
  0.7 0.0 copy-start.3
  0.8 0.1 iota_compare_fusion.15
  0.8 0.6 copy-done.3
  1.4 0.7 select_reduce_fusion
  2.1 6.3 %all-to-all-start = ((s32[4,2,32]{2,1,0:T(2,128)}), s32[4,2,32]{2,1,0:T(2,128)S(1)}, u32[]{:S(2)}, u32[]{:S(2)}) async-start(s32[4,2,32]{2,1,0:T(2,128)} %bitcast.4), calls=%async_computation | async-start | bytes 8192 | tf_op jit(solution)/shard_map/all_to_all | solution.py:99
  8.5 0.0 copy-start.2
  8.5 0.7 copy-done.2
  9.2 0.1 reduce_sum.32
  9.3 0.1 broadcast_divide_fusion
  9.3 0.7 fusion.27
  10.0 1.1 %reshape_squeeze.3 = bf16[4,32768]{1,0:T(4,128)(2,1)S(1)} reshape(bf16[1,4,2,32,512]{4,3,2,1,0:T(8,128)(2,1)} %param.6) | data formatting | bytes 524288 | tf_op jit(solution)/shard_map/reshape;squeeze | solution.py:91
  11.2 0.0 copy-start
  11.2 0.4 convolution_convert_fusion
  11.6 0.3 copy-done
  11.9 0.0 copy-start.1
  11.9 4.7 %all_gather.6 = bf16[1,1,8,16,256]{4,3,1,0,2:T(8,128)(2,1)S(1)} all-gather(bf16[1,1,4,16,256]{4,3,1,0,2:T(8,128)(2,1)S(1)} %bitcast.87), channel_id=1, replica_groups=mesh['region'=2,'tile'=4,'member'=2,'date'=2] {'member'}, dimensions={2}, use_global_device_ids=true | all-gather | bytes 98304 | tf_op jit(solution)/shard_map/all_gather | solution.py:83
  16.7 0.0 copy-done.1
  16.7 4.6 %all_gather.7 = bf16[1,1,8,16,256]{4,3,1,0,2:T(8,128)(2,1)S(1)} all-gather(bf16[1,1,4,16,256]{4,3,1,0,2:T(8,128)(2,1)S(1)} %bitcast.88), channel_id=1, replica_groups=mesh['region'=2,'tile'=4,'member'=2,'date'=2] {'member'}, dimensions={2}, use_global_device_ids=true | all-gather | bytes 98304 | tf_op jit(solution)/shard_map/all_gather | solution.py:84
  21.2 0.1 shift_right_arithmetic.26
  21.3 0.9 %copy.23 = bf16[1,8,64,512]{3,2,1,0:T(8,128)(2,1)} copy(bf16[1,8,64,512]{3,1,2,0:T(8,128)(2,1)S(1)} %bitcast.82) | data formatting | bytes 1048576
  22.3 0.0 all-to-all-done
  22.3 5.1 %all-to-all-start.1 = ((bf16[4,2,2,32,512]{4,3,2,1,0:T(8,128)(2,1)}), bf16[4,2,2,32,512]{4,3,2,1,0:T(8,128)(2,1)S(1)}, u32[]{:S(2)}, u32[]{:S(2)}) async-start(bf16[4,2,2,32,512]{4,3,2,1,0:T(8,128)(2,1)} %bitcast.41), calls=%async_computation.1 | async-start | bytes 1048576 | tf_op jit(solution)/shard_map/all_to_all | solution.py:98
  27.4 0.1 shift_right_arithmetic.23
  27.5 0.1 shift_right_arithmetic.24
  27.6 0.2 copy.17
  27.9 0.1 broadcast_in_dim.101
  28.0 0.4 copy.18
  28.3 10.7 %all-to-all-done.1 = bf16[4,2,2,32,512]{4,3,2,1,0:T(8,128)(2,1)S(1)} async-done(((bf16[4,2,2,32,512]{4,3,2,1,0:T(8,128)(2,1)}), bf16[4,2,2,32,512]{4,3,2,1,0:T(8,128)(2,1)S(1)}, u32[]{:S(2)}, u32[]{:S(2)}) %all-to-all-start.1) | async-done | bytes 524320 | tf_op jit(solution)/shard_map/all_to_all | solution.py:98
  39.0 9.3 %fusion.7 = bf16[8,2,16,256]{3,2,1,0:T(8,128)(2,1)S(1)} fusion(bf16[8,2,32,512]{3,2,1,0:T(8,128)(2,1)S(1)} %bitcast.84, f32[]{:T(128)} %bitcast.27, s32[256]{0:T(256)S(1)} %get-tuple-element.20, f32[]{:T(128)} %bitcast.26, s32[256]{0:T(256)S(1)} %get-tuple-element.21, f32[]{:T(128)} %bitcast.25, s32[256]{0:T(256)S(1)} %get-tuple-element.22, f32[]{:T(128)} %bitcast.24, ...), kind=kOutput, calls=%fused_computation.12 | convolution fusion | flops 78785024 | bytes 1056248 | tf_op jit(solution)/shard_map/...ic,cj->...ij/dot_general | solution.py:49
  48.3 9.3 %convolution_convert_fusion.2 = bf16[8,2,512,32]{2,3,1,0:T(8,128)(2,1)S(1)} fusion(bf16[8,2,16,256]{3,2,1,0:T(8,128)(2,1)S(1)} %fusion.7, f32[]{:T(128)} %bitcast.27, s32[256]{0:T(256)S(1)} %get-tuple-element.20, f32[]{:T(128)} %bitcast.26, s32[256]{0:T(256)S(1)} %get-tuple-element.21, f32[]{:T(128)} %bitcast.25, s32[256]{0:T(256)S(1)} %get-tuple-element.22, ...), kind=kOutput, calls=%fused_computation.2 | convolution fusion | flops 78653952 | bytes 663032 | tf_op jit(solution)/shard_map/ir,...ic->...rc/dot_general | solution.py:58
  57.6 15.5 %all_to_all.15 = bf16[4,2,2,32,512]{4,3,2,1,0:T(8,128)(2,1)S(1)} all-to-all(bf16[4,2,2,32,512]{4,3,2,1,0:T(8,128)(2,1)S(1)} %bitcast.85), channel_id=1, replica_groups=mesh['region'=2,'tile'=4,'member'=2,'date'=2] {'tile'}, dimensions={0} | all-to-all | bytes 1048576 | tf_op jit(solution)/shard_map/all_to_all | solution.py:107
  73.1 0.2 reshape.71
  73.4 0.4 convolution_convert_fusion.1
  73.7 0.7 %copy.24 = bf16[1,4,64,512]{3,2,1,0:T(8,128)(2,1)} copy(bf16[1,4,64,512]{3,1,2,0:T(4,128)(2,1)S(1)} %bitcast.83) | data formatting | bytes 524288
  (15 shorter events, 0.1 us)
Async XLA Ops:
  0.0 0.7 copy-start.4
  0.7 0.7 copy-start.3
  2.1 20.2 %all-to-all-start = ((s32[4,2,32]{2,1,0:T(2,128)}), s32[4,2,32]{2,1,0:T(2,128)S(1)}, u32[]{:S(2)}, u32[]{:S(2)}) async-start(s32[4,2,32]{2,1,0:T(2,128)} %bitcast.4), calls=%async_computation | async-start | bytes 8192 | tf_op jit(solution)/shard_map/all_to_all | solution.py:99
  8.5 0.7 copy-start.2
  11.2 0.8 %copy-start = (bf16[1,1,4,16,256]{4,3,2,1,0:T(8,128)(2,1)S(1)}, bf16[1,1,4,16,256]{4,3,2,1,0:T(8,128)(2,1)}, u32[]{:S(2)}) copy-start(bf16[1,1,4,16,256]{4,3,2,1,0:T(8,128)(2,1)} %param.9) | copy-start | bytes 98308
  11.9 4.7 %copy-start.1 = (bf16[1,1,4,16,256]{4,3,2,1,0:T(8,128)(2,1)S(1)}, bf16[1,1,4,16,256]{4,3,2,1,0:T(8,128)(2,1)}, u32[]{:S(2)}) copy-start(bf16[1,1,4,16,256]{4,3,2,1,0:T(8,128)(2,1)} %param.10) | copy-start | bytes 98308
  22.3 16.7 %all-to-all-start.1 = ((bf16[4,2,2,32,512]{4,3,2,1,0:T(8,128)(2,1)}), bf16[4,2,2,32,512]{4,3,2,1,0:T(8,128)(2,1)S(1)}, u32[]{:S(2)}, u32[]{:S(2)}) async-start(bf16[4,2,2,32,512]{4,3,2,1,0:T(8,128)(2,1)} %bitcast.41), calls=%async_computation.1 | async-start | bytes 1048576 | tf_op jit(solution)/shard_map/all_to_all | solution.py:98
where the time goes:
time: 75.2 us; the launch traced here: 74.5 us
  blocking collectives  24.8 us (33%)
  matrix products  19.4 us (26%)
  starting transfers between devices  11.4 us (15%)
  waiting for transfers between devices  10.7 us (14%)
  local copies, waits for them, and re-layouts  6.98 us (9%)
  other arithmetic  1.09 us (1%)
    all_to_all x1, blocking collectives, per_device(): lax.all_to_all(answered, 'tile', split_axis=0, concat_axis=0, tiled=True)  15.5 us
    all_to_all x1, waiting for transfers between devices, per_device(): lax.all_to_all(outgoing, 'tile', split_axis=0, concat_axis=0, tiled=True)  10.7 us
    dot_general x1, matrix products, degrade(): jnp.einsum('...ic,cj->...ij', blurred, col_table, preferred_element_type=...  9.32 us
    dot_general x1, matrix products, adjoint_map(): jnp.einsum('ir,...ic->...rc', row_table, spread, preferred_element_type=j...  9.32 us
    all_to_all x1, starting transfers between devices, per_device(): lax.all_to_all(words_out, 'tile', split_axis=0, concat_axis=0, tiled=True)  6.32 us
    all_to_all x1, starting transfers between devices, per_device(): lax.all_to_all(outgoing, 'tile', split_axis=0, concat_axis=0, tiled=True)  5.08 us
    all_gather x1, blocking collectives, per_device(): lax.all_gather(scene_lai, 'member', axis=2, tiled=True)  4.71 us
    all_gather x1, blocking collectives, per_device(): lax.all_gather(scene_sigma, 'member', axis=2, tiled=True)  4.58 us
  transfers between devices with their start and end apart: 2, of which 1 were waited for; matrix products, arithmetic and copies ran while one was open for 6% of the time, Pallas kernels for 0%

commit v1 on v0

--- a/solution.py
+++ b/solution.py
@@ -1,9 +1,27 @@
+import functools
 import jax
 import jax.numpy as jnp
 from jax import lax
 from jax.sharding import PartitionSpec as P
 
 CAP = 2
+
+
+def list_terms(body, lane_axis):
+    x_now, val = (lax.axis_size(lane_axis), lax.axis_index(lane_axis))
+    w1, ready = (body, 1)
+    while ready < x_now:
+        tile_out = lax.ppermute(
+            w1, axis_name=lane_axis, perm=[(at, at ^ ready) for at in range(x_now)]
+        )
+        t1 = jnp.concatenate([w1, tile_out], 2)
+        after = jnp.concatenate([tile_out, w1], 2)
+        w1 = jnp.where(val & ready == 0, t1, after)
+        ready = 2 * ready
+    return w1
+
+
+_update_notes = functools.partial(list_terms, lane_axis="member")
 
 
 def band_tables(mtf_taps, tile_rows, tile_cols):
@@ -80,7 +98,7 @@
     slot_onehot = lax.broadcasted_iota(jnp.int32, (slot_count, tiles_here), 0) == target[None, :]
     onehot_bf = slot_onehot.astype(jnp.bfloat16)
     scenes, sigmas = (
-        lax.all_gather(scene_lai, "member", axis=2, tiled=True),
+        _update_notes(scene_lai),
         lax.all_gather(scene_sigma, "member", axis=2, tiled=True),
     )
     local_tiles = sim_lai[0]

time: 75.2 us -> 72.3 us (0.961)
  blocking collectives: 24.8 us -> 20.1 us
  starting transfers between devices: 11.4 us -> 12.9 us
    all_gather x1 -> x0, blocking collectives: 4.71 us -> none  [per_device(): lax.all_gather(scene_lai, 'member', axis=2, tiled=True)]
    ppermute x0 -> x1, starting transfers between devices: none -> 1.49 us  [list_terms(): lax.ppermute(w1, axis_name=lane_axis, perm=[(at, at ^ ready) for at in ra...]
  transfers between devices with their start and end apart: 2 -> 3, of which waited for: 1 -> 1; matrix products, arithmetic and copies ran while one was open for 6% -> 6% of each run, Pallas kernels for 0% -> 0%
where the time goes in v1:
time: 72.3 us; the launch traced here: 71.5 us
  blocking collectives  20.1 us (28%)
  matrix products  19.5 us (27%)
  starting transfers between devices  12.9 us (18%)
  waiting for transfers between devices  10.4 us (14%)
  local copies, waits for them, and re-layouts  7.39 us (10%)
  other arithmetic  1.09 us (2%)
    all_to_all x1, blocking collectives, per_device(): lax.all_to_all(answered, 'tile', split_axis=0, concat_axis=0, tiled=True)  15.5 us
    all_to_all x1, waiting for transfers between devices, per_device(): lax.all_to_all(outgoing, 'tile', split_axis=0, concat_axis=0, tiled=True)  10.4 us
    dot_general x1, matrix products, degrade(): jnp.einsum('...ic,cj->...ij', blurred, col_table, preferred_element_type=...  9.35 us
    dot_general x1, matrix products, adjoint_map(): jnp.einsum('ir,...ic->...rc', row_table, spread, preferred_element_type=j...  9.35 us
    all_to_all x1, starting transfers between devices, per_device(): lax.all_to_all(words_out, 'tile', split_axis=0, concat_axis=0, tiled=True)  6.32 us
    all_to_all x1, starting transfers between devices, per_device(): lax.all_to_all(outgoing, 'tile', split_axis=0, concat_axis=0, tiled=True)  5.09 us
    all_gather x1, blocking collectives, per_device(): lax.all_gather(scene_sigma, 'member', axis=2, tiled=True)  4.58 us
    unnamed x12, local copies, waits for them, and re-layouts  4.37 us
  transfers between devices with their start and end apart: 3, of which 1 were waited for; matrix products, arithmetic and copies ran while one was open for 6% of the time, Pallas kernels for 0%

profile of v1, /device:TPU:0, one launch (start us, length us, event | category | flops | bytes accessed | tf_op | source)
XLA Modules:
  0.0 71.5 jit_solution(306743701810885015)
XLA Ops:
  0.0 0.0 copy-start.4
  0.0 0.7 copy-done.4
  0.7 0.1 convert_reduce_fusion
  0.7 0.0 copy-start.3
  0.8 0.1 iota_compare_fusion.15
  0.8 0.6 copy-done.3
  1.4 0.7 select_reduce_fusion
  2.1 6.3 %all-to-all-start = ((s32[4,2,32]{2,1,0:T(2,128)}), s32[4,2,32]{2,1,0:T(2,128)S(1)}, u32[]{:S(2)}, u32[]{:S(2)}) async-start(s32[4,2,32]{2,1,0:T(2,128)} %bitcast.4), calls=%async_computation | async-start | bytes 8192 | tf_op jit(solution)/shard_map/all_to_all | solution.py:117
  8.4 1.5 %collective-permute-start = (bf16[1,1,4,16,256]{4,3,2,1,0:T(8,128)(2,1)}, bf16[1,1,4,16,256]{4,3,2,1,0:T(8,128)(2,1)S(1)}, u32[]{:S(2)}, u32[]{:S(2)}) collective-permute-start(bf16[1,1,4,16,256]{4,3,2,1,0:T(8,128)(2,1)} %param.9), channel_id=1, source_target_pairs={{0,2},{2,0},{1,3},{3,1},{4,6},{6,4},{5,7},{7,5},{8,10},{10,8},{9,1... | collective-permute-start | bytes 98312 | tf_op jit(solution)/shard_map/ppermute | solution.py:14
  10.0 0.0 copy-start.2
  10.0 0.7 copy-done.2
  10.6 0.1 reduce_sum.32
  10.8 0.1 broadcast_divide_fusion
  10.8 1.1 %reshape_squeeze.3 = bf16[4,32768]{1,0:T(4,128)(2,1)S(1)} reshape(bf16[1,4,2,32,512]{4,3,2,1,0:T(8,128)(2,1)} %param.6) | data formatting | bytes 524288 | tf_op jit(solution)/shard_map/reshape;squeeze | solution.py:109
  12.0 0.0 copy-start
  12.0 0.4 convolution_convert_fusion
  12.4 0.3 copy-done
  12.7 4.6 %all_gather.3 = bf16[1,1,8,16,256]{4,3,1,0,2:T(8,128)(2,1)S(1)} all-gather(bf16[1,1,4,16,256]{4,3,1,0,2:T(8,128)(2,1)S(1)} %bitcast.85), channel_id=1, replica_groups=mesh['region'=2,'tile'=4,'member'=2,'date'=2] {'member'}, dimensions={2}, use_global_device_ids=true | all-gather | bytes 98304 | tf_op jit(solution)/shard_map/all_gather | solution.py:102
  17.3 0.1 shift_right_arithmetic.26
  17.4 1.0 %copy.21 = bf16[1,8,64,512]{3,2,1,0:T(8,128)(2,1)} copy(bf16[1,8,64,512]{3,1,2,0:T(8,128)(2,1)S(1)} %bitcast.80) | data formatting | bytes 1048576
  18.4 0.0 all-to-all-done
  18.4 5.1 %all-to-all-start.1 = ((bf16[4,2,2,32,512]{4,3,2,1,0:T(8,128)(2,1)}), bf16[4,2,2,32,512]{4,3,2,1,0:T(8,128)(2,1)S(1)}, u32[]{:S(2)}, u32[]{:S(2)}) async-start(bf16[4,2,2,32,512]{4,3,2,1,0:T(8,128)(2,1)} %bitcast.40), calls=%async_computation.1 | async-start | bytes 1048576 | tf_op jit(solution)/shard_map/all_to_all | solution.py:116
  23.5 0.7 fusion.28
  24.2 0.1 shift_right_arithmetic.23
  24.3 0.1 shift_right_arithmetic.24
  24.4 0.2 copy.16
  24.7 0.1 broadcast_in_dim.101
  24.7 0.0 copy-start.1
  24.8 0.4 copy.17
  25.1 0.0 collective-permute-done
  25.1 0.4 copy-done.1
  25.5 10.4 %all-to-all-done.1 = bf16[4,2,2,32,512]{4,3,2,1,0:T(8,128)(2,1)S(1)} async-done(((bf16[4,2,2,32,512]{4,3,2,1,0:T(8,128)(2,1)}), bf16[4,2,2,32,512]{4,3,2,1,0:T(8,128)(2,1)S(1)}, u32[]{:S(2)}, u32[]{:S(2)}) %all-to-all-start.1) | async-done | bytes 524320 | tf_op jit(solution)/shard_map/all_to_all | solution.py:116
  36.0 9.4 %fusion.7 = bf16[8,2,16,256]{3,2,1,0:T(8,128)(2,1)S(1)} fusion(bf16[8,2,32,512]{3,2,1,0:T(8,128)(2,1)S(1)} %bitcast.82, f32[]{:T(128)} %bitcast.27, s32[256]{0:T(256)S(1)} %get-tuple-element.19, f32[]{:T(128)} %bitcast.26, s32[256]{0:T(256)S(1)} %get-tuple-element.20, f32[]{:T(128)} %bitcast.25, s32[256]{0:T(256)S(1)} %get-tuple-element.21, f32[]{:T(128)} %bitcast.24, ...), kind=kOutput, calls=%fused_computation.12 | convolution fusion | flops 78785024 | bytes 1056248 | tf_op jit(solution)/shard_map/...ic,cj->...ij/dot_general | solution.py:67
  45.3 9.3 %convolution_convert_fusion.2 = bf16[8,2,512,32]{2,3,1,0:T(8,128)(2,1)S(1)} fusion(bf16[8,2,16,256]{3,2,1,0:T(8,128)(2,1)S(1)} %fusion.7, f32[]{:T(128)} %bitcast.27, s32[256]{0:T(256)S(1)} %get-tuple-element.19, f32[]{:T(128)} %bitcast.26, s32[256]{0:T(256)S(1)} %get-tuple-element.20, f32[]{:T(128)} %bitcast.25, s32[256]{0:T(256)S(1)} %get-tuple-element.21, ...), kind=kOutput, calls=%fused_computation.2 | convolution fusion | flops 78653952 | bytes 663032 | tf_op jit(solution)/shard_map/ir,...ic->...rc/dot_general | solution.py:76
  54.7 15.5 %all_to_all.15 = bf16[4,2,2,32,512]{4,3,2,1,0:T(8,128)(2,1)S(1)} all-to-all(bf16[4,2,2,32,512]{4,3,2,1,0:T(8,128)(2,1)S(1)} %bitcast.83), channel_id=1, replica_groups=mesh['region'=2,'tile'=4,'member'=2,'date'=2] {'tile'}, dimensions={0} | all-to-all | bytes 1048576 | tf_op jit(solution)/shard_map/all_to_all | solution.py:125
  70.2 0.2 reshape.119
  70.4 0.3 convolution_convert_fusion.1
  70.8 0.7 %copy.22 = bf16[1,4,64,512]{3,2,1,0:T(8,128)(2,1)} copy(bf16[1,4,64,512]{3,1,2,0:T(4,128)(2,1)S(1)} %bitcast.81) | data formatting | bytes 524288
  (15 shorter events, 0.1 us)
Async XLA Ops:
  0.0 0.7 copy-start.4
  0.7 0.7 copy-start.3
  2.1 16.3 %all-to-all-start = ((s32[4,2,32]{2,1,0:T(2,128)}), s32[4,2,32]{2,1,0:T(2,128)S(1)}, u32[]{:S(2)}, u32[]{:S(2)}) async-start(s32[4,2,32]{2,1,0:T(2,128)} %bitcast.4), calls=%async_computation | async-start | bytes 8192 | tf_op jit(solution)/shard_map/all_to_all | solution.py:117
  8.4 16.7 %collective-permute-start = (bf16[1,1,4,16,256]{4,3,2,1,0:T(8,128)(2,1)}, bf16[1,1,4,16,256]{4,3,2,1,0:T(8,128)(2,1)S(1)}, u32[]{:S(2)}, u32[]{:S(2)}) collective-permute-start(bf16[1,1,4,16,256]{4,3,2,1,0:T(8,128)(2,1)} %param.9), channel_id=1, source_target_pairs={{0,2},{2,0},{1,3},{3,1},{4,6},{6,4},{5,7},{7,5},{8,10},{10,8},{9,1... | collective-permute-start | bytes 98312 | tf_op jit(solution)/shard_map/ppermute | solution.py:14
  10.0 0.7 copy-start.2
  12.0 0.8 %copy-start = (bf16[1,1,4,16,256]{4,3,2,1,0:T(8,128)(2,1)S(1)}, bf16[1,1,4,16,256]{4,3,2,1,0:T(8,128)(2,1)}, u32[]{:S(2)}) copy-start(bf16[1,1,4,16,256]{4,3,2,1,0:T(8,128)(2,1)} %param.10) | copy-start | bytes 98308
  18.4 17.6 %all-to-all-start.1 = ((bf16[4,2,2,32,512]{4,3,2,1,0:T(8,128)(2,1)}), bf16[4,2,2,32,512]{4,3,2,1,0:T(8,128)(2,1)S(1)}, u32[]{:S(2)}, u32[]{:S(2)}) async-start(bf16[4,2,2,32,512]{4,3,2,1,0:T(8,128)(2,1)} %bitcast.40), calls=%async_computation.1 | async-start | bytes 1048576 | tf_op jit(solution)/shard_map/all_to_all | solution.py:116
  24.7 0.8 %copy-start.1 = (bf16[1,1,4,16,256]{4,3,2,1,0:T(8,128)(2,1)S(1)}, bf16[1,1,4,16,256]{4,3,2,1,0:T(8,128)(2,1)}, u32[]{:S(2)}) copy-start(bf16[1,1,4,16,256]{4,3,2,1,0:T(8,128)(2,1)} %param.9) | copy-start | bytes 98308
